TPU v7x, 512 devices: a whole 4x4x16 slice. The times are simulated.
512 devices in a mesh: chan: 8 (over y, x_lo), tile: 64 (over z, x_hi, core).
Axes of the slice: x: 4 (x_hi: 2, x_lo: 2; x = x_hi * 2 + x_lo), y: 4, z: 16, core: 2. Of those that a mesh axis runs over, the one named last changes fastest.
Arguments:
- image: bfloat16 [256, 1024, 256], P('chan', 'tile'), may hold values from -6 to 6
- w_down: bfloat16 [2, 2, 256, 512], P(None, None, None, 'chan'), may hold values from -0.1875 to 0.1875
- w_mix: bfloat16 [3, 3, 512, 512], P(None, None, None, 'chan'), may hold values from -0.09375 to 0.09375
- cotangent: bfloat16 [512, 512, 128], P('chan', 'tile'), may hold values from -6 to 6
Outputs:
- mixed: bfloat16 [512, 512, 128], P('chan', 'tile')
- grad_mix: float32 [512, 3, 3, 512], P('tile', None, None, 'chan')
- grad_down: float32 [256, 2, 2, 512], P('tile', None, None, 'chan')
- grad_image: bfloat16 [256, 1024, 256], P('chan', 'tile')
All inputs are finite; a program needn't handle non-finite values.
Results may differ from a plain program's by a relative error of at most 0.0049.
Values may be sent and summed in bfloat16 or wider, within the bound.
No kernel may reach another device: no remote copies, remote signals or barrier semaphores. Data moves between devices by JAX's collectives and lax.ppermute only.
A program may use at most 64 MiB of HBM per device.

v0:
```python
import math
import jax
import jax.numpy as jnp
from jax import lax
from jax.sharding import PartitionSpec as P


def with_halo(block, sides, width):
    for axis, dim in sides:
        count = lax.axis_size(axis)
        forward = [(i, i + 1) for i in range(count - 1)]
        backward = [(target, source) for source, target in forward]
        low = lax.ppermute(
            lax.slice_in_dim(block, block.shape[dim] - width, None, axis=dim), axis, forward
        )
        high = lax.ppermute(lax.slice_in_dim(block, 0, width, axis=dim), axis, backward)
        block = jnp.concatenate([low, block, high], axis=dim)
    return block


def normal_cdf(value):
    return 0.5 * (1.0 + jax.scipy.special.erf(value / math.sqrt(2.0)))


def normal_pdf(value):
    return jnp.exp(-0.5 * value * value) / math.sqrt(2.0 * math.pi)


def per_device(image, w_down, w_mix, cotangent):
    n_tile = lax.axis_size("tile")
    own_out = cotangent.shape[0]
    n_rows = cotangent.shape[1]
    n_cols = cotangent.shape[2]
    own_in = image.shape[0]
    scale = 1.0 / math.sqrt(n_rows * n_tile * n_cols)
    wide_image = lax.all_gather(image, "chan", axis=0, tiled=True)
    in_chan = wide_image.shape[0]
    patches = wide_image.reshape(in_chan, n_rows, 2, n_cols, 2)
    preact = jnp.einsum("crawb,abcd->drw", patches, w_down, preferred_element_type=jnp.float32)
    hidden = (preact * normal_cdf(preact)).astype(jnp.bfloat16)
    plain = lax.all_gather(hidden, "chan", axis=0, tiled=True)
    full_hidden = with_halo(plain, (("tile", 1),), 1)
    hidden_pad = jnp.pad(full_hidden, ((0, 0), (0, 0), (1, 1)))
    all_chan = hidden_pad.shape[0]
    mixed_sum = jnp.zeros((own_out, n_rows, n_cols), jnp.float32)
    for tap_row in range(3):
        for tap_col in range(3):
            window = hidden_pad[:, tap_row : tap_row + n_rows, tap_col : tap_col + n_cols]
            mixed_sum = mixed_sum + jnp.einsum(
                "crw,cd->drw", window, w_mix[tap_row, tap_col], preferred_element_type=jnp.float32
            )
    mixed = mixed_sum.astype(jnp.bfloat16)
    cot_rimmed = with_halo(cotangent, (("tile", 1),), 1)
    part = hidden_pad
    terms = []
    for tap_row in range(3):
        for tap_col in range(3):
            window = part[:, tap_row : tap_row + n_rows, tap_col : tap_col + n_cols]
            terms.append(
                jnp.einsum("crw,drw->cd", window, cotangent, preferred_element_type=jnp.float32)
            )
    grad_mix = (
        lax.psum_scatter(
            jnp.stack(terms, 1).reshape(all_chan // n_tile * lax.axis_size("tile"), 3, 3, own_out),
            "tile",
            scatter_dimension=0,
            tiled=True,
        )
        * scale
    )
    cot_pad = jnp.pad(cot_rimmed, ((0, 0), (0, 0), (1, 1)))
    total = jnp.zeros((own_out * lax.axis_size("chan"), n_rows, n_cols), jnp.float32)
    for tap_row in range(3):
        for tap_col in range(3):
            back = cot_pad[
                :, 2 - tap_row : 2 - tap_row + n_rows, 2 - tap_col : 2 - tap_col + n_cols
            ]
            filters = w_mix[tap_row, tap_col]
            total = total + jnp.einsum(
                "drw,cd->crw", back, filters, preferred_element_type=jnp.float32
            )
    grad_hidden = lax.psum_scatter(total, "chan", scatter_dimension=0, tiled=True)
    slope = normal_cdf(preact) + preact * normal_pdf(preact)
    grad_pre = (grad_hidden * slope).astype(jnp.bfloat16)
    part = patches
    grad_down = (
        lax.psum_scatter(
            jnp.einsum("crawb,drw->cabd", part, grad_pre, preferred_element_type=jnp.float32),
            "tile",
            scatter_dimension=0,
            tiled=True,
        )
        * scale
    )
    down_turned = lax.all_to_all(w_down, "chan", split_axis=2, concat_axis=3, tiled=True)
    filters = down_turned
    term = jnp.einsum(
        "drw,abcd->crawb",
        lax.all_gather(grad_pre, "chan", axis=0, tiled=True),
        filters,
        preferred_element_type=jnp.float32,
    )
    grad_image = term.reshape(jnp.zeros((own_in, 2 * n_rows, 2 * n_cols), jnp.float32).shape)
    return (mixed, grad_mix, grad_down, grad_image.astype(jnp.bfloat16))


def solution(mesh):
    return jax.shard_map(
        per_device,
        mesh=mesh,
        in_specs=(
            P("chan", "tile", None),
            P(None, None, None, "chan"),
            P(None, None, None, "chan"),
            P("chan", "tile", None),
        ),
        out_specs=(
            P("chan", "tile", None),
            P("tile", None, None, "chan"),
            P("tile", None, None, "chan"),
            P("chan", "tile", None),
        ),
        check_vma=False,
    )
```

profile of v0, /device:TPU:8, one launch (start us, length us, event | category | flops | bytes accessed | tf_op | source)
XLA Modules:
  0.0 1003.0 jit_solution(11535265165605964177)
XLA Ops:
  8.9 1.7 collective-permute-start.2
  11.9 1.4 fusion.96
  13.4 3.2 collective-permute-done.3
  20.2 2.6 bitcast_add_fusion
  22.9 49.7 %all-gather.4.cloned.1.call-done = bf16[256,16,256]{2,1,0:T(8,128)(2,1)} async-done(((bf16[32,16,256]{2,1,0:T(8,128)(2,1)}), bf16[256,16,256]{2,1,0:T(8,128)(2,1)}) %all-gather.4.cloned.1.call-update) | async-done | bytes 2097168 | tf_op jit(solution)/shard_map/all_gather | solution.py:36
  72.6 3.0 copy.69
  75.6 2.2 reshape.16
  77.8 2.5 fusion.11
  80.3 54.6 %reduce-scatter.5.cloned.1.call-done = f32[64,8,128]{2,0,1:T(8,128)} async-done(((f32[512,8,128]{2,0,1:T(8,128)}), f32[64,8,128]{2,0,1:T(8,128)}) %reduce-scatter.5.cloned.1.call-update) | async-done | bytes 262160 | tf_op jit(solution)/shard_map/reduce_scatter | solution.py:82
  134.9 1.7 fusion.66
  140.4 5.5 all-to-all-start
  147.8 3.2 all-to-all-done
  151.6 511.6 %all-reduce.5.cloned.1.call-done = f32[256,2,2,64]{3,2,1,0:T(2,128)} async-done(((f32[256,2,2,64]{3,2,1,0:T(2,128)}), f32[256,2,2,64]{3,2,1,0:T(2,128)}) %all-reduce.5.cloned.1.call-update) | async-done | bytes 262160
  663.2 1.3 dynamic-slice_multiply_fusion
  664.5 47.3 %all-gather.6.cloned.1.call-done = bf16[512,8,128]{2,0,1:T(8,128)(2,1)} async-done(((bf16[64,8,128]{2,0,1:T(8,128)(2,1)}), bf16[512,8,128]{2,0,1:T(8,128)(2,1)}) %all-gather.6.cloned.1.call-update) | async-done | bytes 1048592 | tf_op jit(solution)/shard_map/all_gather | solution.py:41
  711.9 1.6 fusion.138
  713.5 1.4 collective-permute-start
  714.9 1.5 collective-permute-start.1
  716.4 45.3 %all-gather.8.cloned.1.call-done = bf16[512,8,128]{2,0,1:T(8,128)(2,1)} async-done(((bf16[64,8,128]{2,0,1:T(8,128)(2,1)}), bf16[512,8,128]{2,0,1:T(8,128)(2,1)}) %all-gather.8.cloned.1.call-update) | async-done | bytes 1048592 | tf_op jit(solution)/shard_map/all_gather | solution.py:99
  761.7 1.5 fusion.10
  766.2 2.9 fusion.5
  777.9 2.9 copy.80
  784.8 209.9 %reduce-scatter.3.cloned.1.call-done = f32[8,3,3,64]{3,0,2,1:T(8,128)} async-done(((f32[512,3,3,64]{3,0,2,1:T(8,128)}), f32[8,3,3,64]{3,0,2,1:T(8,128)}) %reduce-scatter.3.cloned.1.call-update) | async-done | bytes 18448 | tf_op jit(solution)/shard_map/reduce_scatter | solution.py:63
  994.7 1.4 broadcast_multiply_fusion
  (85 shorter events, 27.7 us)
Async XLA Ops:
  7.2 9.6 copy-start.5
  7.2 65.4 %all-gather.4.cloned.1.call-start = ((), (), s32[]{:S(2)}) async-start(), calls=%async_computation.3 | async-start | bytes 2359296 | tf_op jit(solution)/shard_map/all_gather | solution.py:36
  7.9 127.0 %reduce-scatter.5.cloned.1.call-start = ((), (), s32[]{:S(2)}) async-start(), calls=%async_computation.6 | async-start | bytes 2359296 | tf_op jit(solution)/shard_map/reduce_scatter | solution.py:82
  8.9 4.4 collective-permute-start.2
  10.6 5.9 collective-permute-start.3
  22.8 640.4 %all-reduce.5.cloned.1.call-start = ((), (), s32[]{:S(2)}) async-start(), calls=%async_computation.8 | async-start | bytes 1048576
  75.6 2.2 copy-start.12
  77.8 58.9 %copy-start.6 = (bf16[256,8,2,128,2]{0,4,3,2,1:T(2,128)(2,1)S(1)}, bf16[256,8,2,128,2]{0,4,3,2,1:T(2,128)(2,1)}, u32[]{:S(2)}) copy-start(bf16[256,8,2,128,2]{0,4,3,2,1:T(2,128)(2,1)} %reshape.16) | copy-start | bytes 6291460
  136.7 2.1 copy-start.11
  138.2 573.7 %all-gather.6.cloned.1.call-start = ((), (), s32[]{:S(2)}) async-start(), calls=%async_computation.4 | async-start | bytes 1179648 | tf_op jit(solution)/shard_map/all_gather | solution.py:41
  138.8 623.0 %all-gather.8.cloned.1.call-start = ((), (), s32[]{:S(2)}) async-start(), calls=%async_computation.7 | async-start | bytes 1179648 | tf_op jit(solution)/shard_map/all_gather | solution.py:99
  140.4 10.6 %all-to-all-start = ((bf16[8,2,4096]{2,1,0:T(2,128)(2,1)}), bf16[8,2,4096]{2,1,0:T(2,128)(2,1)S(1)}, u32[]{:S(2)}, u32[]{:S(2)}) async-start(bf16[8,2,4096]{2,1,0:T(2,128)(2,1)} %reshape.44), calls=%async_computation.2 | async-start | bytes 262144 | tf_op jit(solution)/shard_map/all_to_all | solution.py:95
  145.9 848.8 %reduce-scatter.3.cloned.1.call-start = ((), (), s32[]{:S(2)}) async-start(), calls=%async_computation.5 | async-start | bytes 2396160 | tf_op jit(solution)/shard_map/reduce_scatter | solution.py:63
  713.5 51.7 %copy-start = (bf16[512,8,128]{2,0,1:T(8,128)(2,1)S(1)}, bf16[512,8,128]{2,0,1:T(8,128)(2,1)}, u32[]{:S(2)}) copy-start(bf16[512,8,128]{2,0,1:T(8,128)(2,1)} %all-gather.6.cloned.1.call-done) | copy-start | bytes 3145732
  713.5 52.0 %collective-permute-start = (bf16[512,1,128]{2,0,1:T(8,128)(2,1)}, bf16[512,1,128]{2,0,1:T(8,128)(2,1)S(1)}, u32[]{:S(2)}, u32[]{:S(2)}) collective-permute-start(bf16[512,1,128]{2,0,1:T(8,128)(2,1)} %get-tuple-element.18), channel_id=1, source_target_pairs={{0,1},{1,2},{2,3},{3,4},{4,5},{5,6},{6,7},{7,8},{8,9},{9,10},{10,1... | collective-permute-start | bytes 393224 | tf_op jit(solution)/shard_map/ppermute | solution.py:13
  714.9 51.3 %collective-permute-start.1 = (bf16[512,1,128]{2,0,1:T(8,128)(2,1)S(1)}, bf16[512,1,128]{2,0,1:T(8,128)(2,1)}, u32[]{:S(2)}, u32[]{:S(2)}) collective-permute-start(bf16[512,1,128]{2,0,1:T(8,128)(2,1)S(1)} %get-tuple-element.19), channel_id=1, source_target_pairs={{1,0},{2,1},{3,2},{4,3},{5,4},{6,5},{7,6},{8,7},{9,8},{10,9},{11,1... | collective-permute-start | bytes 393224 | tf_op jit(solution)/shard_map/ppermute | solution.py:16
  765.5 3.6 copy-start.4
  765.5 4.1 copy-start.1
  765.5 0.7 copy-start.9
  766.2 3.4 copy-start.10
  774.8 1.0 copy-start.2
  776.8 1.0 copy-start.7
  780.8 1.3 copy-start.3
  782.0 1.2 copy-start.8
Sparse Core Ops, SparseCore 0:
  10.1 62.4 all-gather.3
  75.4 59.4 reduce-scatter.4
  138.3 524.8 all-reduce.4
  665.9 45.8 all-gather.5
  714.0 47.6 all-gather.7
  780.9 213.8 reduce-scatter.2
where the time goes:
time: 1000 us
  waiting for transfers between devices  927 us (93%)
  local copies, waits for them, and re-layouts  21.7 us (2%)
  matrix products  20.4 us (2%)
  between operations  15.1 us (2%)
  starting transfers between devices  11.6 us (1%)
    unnamed x7, waiting for transfers between devices  513 us
    reduce_scatter x1, waiting for transfers between devices, per_device(): lax.psum_scatter(jnp.stack(terms, 1).reshape(all_chan // n_tile * lax.axi...  210 us
    reduce_scatter x1, waiting for transfers between devices, per_device(): lax.psum_scatter(total, 'chan', scatter_dimension=0, tiled=True)  54.6 us
    all_gather x1, waiting for transfers between devices, per_device(): wide_image = lax.all_gather(image, 'chan', axis=0, tiled=True)  49.7 us
    all_gather x1, waiting for transfers between devices, per_device(): plain = lax.all_gather(hidden, 'chan', axis=0, tiled=True)  47.3 us
    all_gather x1, waiting for transfers between devices, per_device(): lax.all_gather(grad_pre, 'chan', axis=0, tiled=True)  45.3 us
  transfers between devices with their start and end apart: 11, of which 8 were waited for; matrix products, arithmetic and copies ran while one was open for 3% of the time, Pallas kernels for 0%

commit v1 on v0

--- a/solution.py
+++ b/solution.py
@@ -3,6 +3,12 @@
 import jax.numpy as jnp
 from jax import lax
 from jax.sharding import PartitionSpec as P
+
+
+def _load_tasks(w_in):
+    all_rows = jnp.stack([w_in for _ in range(jax.lax.axis_size("chan"))])
+    row_out = jax.lax.all_to_all(all_rows, "chan", 0, 0)
+    return jnp.concatenate(row_out, 0)
 
 
 def with_halo(block, sides, width):
@@ -95,10 +101,7 @@
     down_turned = lax.all_to_all(w_down, "chan", split_axis=2, concat_axis=3, tiled=True)
     filters = down_turned
     term = jnp.einsum(
-        "drw,abcd->crawb",
-        lax.all_gather(grad_pre, "chan", axis=0, tiled=True),
-        filters,
-        preferred_element_type=jnp.float32,
+        "drw,abcd->crawb", _load_tasks(grad_pre), filters, preferred_element_type=jnp.float32
     )
     grad_image = term.reshape(jnp.zeros((own_in, 2 * n_rows, 2 * n_cols), jnp.float32).shape)
     return (mixed, grad_mix, grad_down, grad_image.astype(jnp.bfloat16))

time: 1000 us -> 960 us (0.960)
  waiting for transfers between devices: 927 us -> 877 us
  blocking collectives: 0 us -> 10.3 us
    all_gather x1 -> x0, waiting for transfers between devices: 45.3 us -> none  [per_device(): lax.all_gather(grad_pre, 'chan', axis=0, tiled=True)]
    all_to_all x0 -> x1, blocking collectives: none -> 10.3 us  [per_device(): lax.all_to_all(w_down, 'chan', split_axis=2, concat_axis=3, tiled=True)]
    unnamed x7 -> x6, waiting for transfers between devices: 513 us -> 507 us
  transfers between devices with their start and end apart: 11 -> 10, of which waited for: 8 -> 7; matrix products, arithmetic and copies ran while one was open for 3% -> 3% of each run, Pallas kernels for 0% -> 0%
where the time goes in v1:
time: 960 us
  waiting for transfers between devices  877 us (91%)
  matrix products  20.4 us (2%)
  local copies, waits for them, and re-layouts  19.7 us (2%)
  between operations  14.8 us (2%)
  starting transfers between devices  11.1 us (1%)
  blocking collectives  10.3 us (1%)
    unnamed x6, waiting for transfers between devices  507 us
    reduce_scatter x1, waiting for transfers between devices, per_device(): lax.psum_scatter(jnp.stack(terms, 1).reshape(all_chan // n_tile * lax.axi...  215 us
    reduce_scatter x1, waiting for transfers between devices, per_device(): lax.psum_scatter(total, 'chan', scatter_dimension=0, tiled=True)  54.7 us
    all_gather x1, waiting for transfers between devices, per_device(): wide_image = lax.all_gather(image, 'chan', axis=0, tiled=True)  49.7 us
    all_gather x1, waiting for transfers between devices, per_device(): plain = lax.all_gather(hidden, 'chan', axis=0, tiled=True)  45 us
  transfers between devices with their start and end apart: 10, of which 7 were waited for; matrix products, arithmetic and copies ran while one was open for 3% of the time, Pallas kernels for 0%

profile of v1, /device:TPU:8, one launch (start us, length us, event | category | flops | bytes accessed | tf_op | source)
XLA Modules:
  0.0 959.6 jit_solution(10420794715732392122)
XLA Ops:
  8.9 1.7 collective-permute-start.2
  10.6 1.3 collective-permute-start.3
  11.9 1.4 fusion.97
  13.4 3.2 collective-permute-done.3
  20.2 2.6 bitcast_add_fusion
  22.9 49.7 %all-gather.3.cloned.1.call-done = bf16[256,16,256]{2,1,0:T(8,128)(2,1)} async-done(((bf16[32,16,256]{2,1,0:T(8,128)(2,1)}), bf16[256,16,256]{2,1,0:T(8,128)(2,1)}) %all-gather.3.cloned.1.call-update) | async-done | bytes 2097168 | tf_op jit(solution)/shard_map/all_gather | solution.py:42
  72.6 3.0 copy.68
  75.6 2.2 reshape.19
  77.8 2.5 fusion.12
  80.3 54.7 %reduce-scatter.5.cloned.1.call-done = f32[64,8,128]{2,0,1:T(8,128)} async-done(((f32[512,8,128]{2,0,1:T(8,128)}), f32[64,8,128]{2,0,1:T(8,128)}) %reduce-scatter.5.cloned.1.call-update) | async-done | bytes 262160 | tf_op jit(solution)/shard_map/reduce_scatter | solution.py:88
  134.9 1.7 fusion.67
  139.2 10.3 %all_to_all.20 = bf16[8,2,4096]{2,1,0:T(2,128)(2,1)S(1)} all-to-all(bf16[8,2,4096]{2,1,0:T(2,128)(2,1)S(1)} %reshape.47), channel_id=1, replica_groups=mesh['chan'=8,'tile'=64] {'chan'}, dimensions={0} | all-to-all | bytes 262144 | tf_op jit(solution)/shard_map/all_to_all | solution.py:101
  150.7 5.1 all-to-all-start
  158.0 505.2 %all-reduce.5.cloned.1.call-done = f32[256,2,2,64]{3,2,1,0:T(2,128)} async-done(((f32[256,2,2,64]{3,2,1,0:T(2,128)}), f32[256,2,2,64]{3,2,1,0:T(2,128)}) %all-reduce.5.cloned.1.call-update) | async-done | bytes 262160
  663.2 1.3 dynamic-slice_multiply_fusion
  666.8 45.0 %all-gather.5.cloned.1.call-done = bf16[512,8,128]{2,0,1:T(8,128)(2,1)} async-done(((bf16[64,8,128]{2,0,1:T(8,128)(2,1)}), bf16[512,8,128]{2,0,1:T(8,128)(2,1)}) %all-gather.5.cloned.1.call-update) | async-done | bytes 1048592 | tf_op jit(solution)/shard_map/all_gather | solution.py:47
  712.9 1.3 collective-permute-start
  714.3 1.5 collective-permute-start.1
  715.7 1.5 fusion.99
  717.3 3.1 collective-permute-done.1
  720.4 1.8 fusion.5
  730.0 2.8 copy.79
  736.9 214.8 %reduce-scatter.3.cloned.1.call-done = f32[8,3,3,64]{3,0,2,1:T(8,128)} async-done(((f32[512,3,3,64]{3,0,2,1:T(8,128)}), f32[8,3,3,64]{3,0,2,1:T(8,128)}) %reduce-scatter.3.cloned.1.call-update) | async-done | bytes 18448 | tf_op jit(solution)/shard_map/reduce_scatter | solution.py:69
  951.7 1.4 broadcast_multiply_fusion
  (74 shorter events, 25.7 us)
Async XLA Ops:
  7.2 9.6 copy-start.4
  7.2 65.4 %all-gather.3.cloned.1.call-start = ((), (), s32[]{:S(2)}) async-start(), calls=%async_computation.4 | async-start | bytes 2359296 | tf_op jit(solution)/shard_map/all_gather | solution.py:42
  7.9 127.0 %reduce-scatter.5.cloned.1.call-start = ((), (), s32[]{:S(2)}) async-start(), calls=%async_computation.7 | async-start | bytes 2359296 | tf_op jit(solution)/shard_map/reduce_scatter | solution.py:88
  8.9 4.4 collective-permute-start.2
  10.6 5.9 collective-permute-start.3
  22.8 640.4 %all-reduce.5.cloned.1.call-start = ((), (), s32[]{:S(2)}) async-start(), calls=%async_computation.8 | async-start | bytes 1048576
  75.6 2.2 copy-start.8
  77.8 58.9 %copy-start.5 = (bf16[256,8,2,128,2]{0,4,3,2,1:T(2,128)(2,1)S(1)}, bf16[256,8,2,128,2]{0,4,3,2,1:T(2,128)(2,1)}, u32[]{:S(2)}) copy-start(bf16[256,8,2,128,2]{0,4,3,2,1:T(2,128)(2,1)} %reshape.19) | copy-start | bytes 6291460
  138.2 573.7 %all-gather.5.cloned.1.call-start = ((), (), s32[]{:S(2)}) async-start(), calls=%async_computation.5 | async-start | bytes 1179648 | tf_op jit(solution)/shard_map/all_gather | solution.py:47
  150.7 513.8 %all-to-all-start = ((bf16[8,64,8,128]{3,1,2,0:T(8,128)(2,1)}), bf16[8,64,8,128]{3,1,2,0:T(8,128)(2,1)S(1)}, u32[]{:S(2)}, u32[]{:S(2)}) async-start(bf16[8,64,8,128]{3,1,2,0:T(8,128)(2,1)} %stack.51), calls=%async_computation.2 | async-start | bytes 2097152 | tf_op jit(solution)/shard_map/all_to_all | solution.py:10
  155.8 795.9 %reduce-scatter.3.cloned.1.call-start = ((), (), s32[]{:S(2)}) async-start(), calls=%async_computation.6 | async-start | bytes 2396160 | tf_op jit(solution)/shard_map/reduce_scatter | solution.py:69
  711.9 8.5 copy-start
  712.9 4.3 collective-permute-start
  714.3 6.2 collective-permute-start.1
  717.3 4.9 copy-start.3
  726.9 1.0 copy-start.1
  728.9 1.0 copy-start.6
  732.8 1.3 copy-start.2
  734.1 1.2 copy-start.7
Sparse Core Ops, SparseCore 0:
  10.1 62.4 all-gather.2
  75.4 59.4 reduce-scatter.4
  138.3 524.8 all-reduce.4
  666.0 45.8 all-gather.4
  732.9 218.7 reduce-scatter.2
